TPU v7x, 32 devices: a whole 2x2x4 slice. The times are simulated.
32 devices in a mesh: ctx: 2 (over core), head: 4 (over y, x), rep: 4 (over z).
Axes of the slice: x: 2, y: 2, z: 4, core: 2. Of those that a mesh axis runs over, the one named last changes fastest.
Arguments:
- queries: bfloat16 [4096, 2048], P(('rep', 'ctx'), 'head'), parts along dimension 0, may hold values from -9 to 9
- keys: bfloat16 [4096, 2048], P(('rep', 'ctx'), 'head'), parts along dimension 0, may hold values from -9 to 9
- values: bfloat16 [4096, 2048], P(('rep', 'ctx'), 'head'), parts along dimension 0, may hold values from -6 to 6
- out_weight: bfloat16 [2048, 4096], P('head', 'ctx'), may hold values from -0.125 to 0.125
- out_grad: bfloat16 [4096, 4096], P(('rep', 'ctx')), parts along dimension 0, may hold values from -6 to 6
Outputs:
- layer_out: bfloat16 [4096, 4096], P(('rep', 'ctx'), 'head'), parts along dimension 0
- query_grad: bfloat16 [4096, 2048], P(('rep', 'ctx'), 'head'), parts along dimension 0
- key_grad: bfloat16 [4096, 2048], P(('rep', 'ctx'), 'head'), parts along dimension 0
- value_grad: bfloat16 [4096, 2048], P(('rep', 'ctx'), 'head'), parts along dimension 0
- weight_grad: float32 [8192, 4096], P(('rep', 'head'), 'ctx'), parts along dimension 0
There are 4 independent parts, one for each index of `rep`. A program takes and returns all parts, laid end to end along the dimension named above; an argument that names none is the same for every part. Nothing has to cross between parts.
All inputs are finite; a program needn't handle non-finite values.
Results may differ from a plain program's by a relative error of at most 0.012.
Values may be sent and summed in bfloat16 or wider, within the bound.
No kernel may reach another device: no remote copies, remote signals or barrier semaphores. Data moves between devices by JAX's collectives and lax.ppermute only.
A program may use at most 128 MiB of HBM per device.

v0:
```python
import jax
import jax.numpy as jnp
from jax import lax
from jax.sharding import PartitionSpec as P

DH = 128
TILE = 128


EPS = 1e-06
HIGH = lax.Precision.HIGHEST


def entering(array, axis, combine, identity):
    count, here = (lax.axis_size(axis), lax.axis_index(axis))
    everything = lax.all_gather(array.astype(jnp.bfloat16), axis)
    start = jnp.broadcast_to(jnp.asarray(identity, array.dtype), array.shape)

    def step(k, before):
        reached = k < here
        new = combine(before, everything[k].astype(array.dtype))
        return jnp.where(reached, new, before)

    return lax.fori_loop(0, count, step, start)


def entering_2(array, axis, join, neutral):
    count = lax.axis_size(axis)
    place = lax.axis_index(axis)
    ahead = count - 1 - place
    gathered = lax.all_gather(
        array.astype(jnp.bfloat16 if array.dtype == jnp.float32 else array.dtype), axis
    )
    state = jnp.zeros_like(array) + jnp.asarray(neutral, array.dtype)

    def one(step, state):
        source = count - 1 - step
        return join(state, lax.dynamic_index_in_dim(gathered, source, 0, False).astype(array.dtype))

    return lax.fori_loop(0, ahead, one, state)


def feature(x):
    return jax.nn.elu(x) + 1.0


def feature_slope(x):
    return jnp.where(x > 0, 1.0, jnp.exp(jnp.minimum(x, 0.0)))


def tile_normed(fq, fk, vals, prefix):
    tile = fq.shape[1]
    lower = jnp.tril(jnp.ones((tile, tile), jnp.float32))
    scores = jnp.einsum("nthd,nshd->nhts", fq, fk, precision=HIGH) * lower
    raw = jnp.einsum("nhts,nshe->nthe", scores, vals, precision=HIGH)
    raw = raw + jnp.einsum("nthd,nhde->nthe", fq, prefix, precision=HIGH)
    meansq = jnp.mean(raw * raw, axis=-1, keepdims=True)
    return raw * lax.rsqrt(meansq + EPS)


def body(queries, keys, values, out_weight, out_grad):
    tok, local_width = queries.shape
    local_heads = local_width // DH
    tiles = tok // TILE
    shape4 = (tiles, TILE, local_heads, DH)
    q_float = queries.astype(jnp.float32)
    k_float = keys.astype(jnp.float32)
    fq = feature(q_float).reshape(shape4)
    fk = feature(k_float).reshape(shape4)
    v_float = values.astype(jnp.float32).reshape(shape4)
    states = jnp.einsum("nshd,nshe->nhde", fk, v_float, precision=HIGH)
    local_sum = jnp.sum(states, 0)
    nothing = jnp.zeros_like(local_sum)
    carried = entering(local_sum, "ctx", jnp.add, nothing)
    prefix = carried[None] + (jnp.cumsum(states, 0) - states)
    normed, pull = jax.vjp(tile_normed, fq, fk, v_float, prefix)
    attn = normed.reshape(tok, local_width).astype(jnp.bfloat16)
    partial_out = jnp.dot(
        attn,
        lax.all_gather(out_weight, "ctx", axis=1, tiled=True),
        preferred_element_type=jnp.float32,
    )
    layer_out = lax.psum_scatter(
        partial_out.astype(jnp.bfloat16), "head", scatter_dimension=1, tiled=True
    )
    contract_cols = (((1,), (1,)), ((), ()))
    attn_grad = lax.dot_general(
        out_grad,
        lax.all_gather(out_weight, "ctx", axis=1, tiled=True),
        contract_cols,
        preferred_element_type=jnp.float32,
    ).astype(jnp.bfloat16)
    term = lax.dot_general(
        attn, out_grad, (((0,), (0,)), ((), ())), preferred_element_type=jnp.float32
    )
    weight_grad = lax.psum_scatter(
        term.astype(jnp.bfloat16), "ctx", scatter_dimension=1, tiled=True
    ).astype(jnp.float32)
    cotangent = attn_grad.astype(jnp.float32).reshape(shape4)
    grad_fq, grad_fk, grad_v, grad_prefix = pull(cotangent)
    later = jnp.sum(grad_prefix, 0)
    suffix = entering_2(later, "ctx", jnp.add, nothing)
    grad_states = suffix[None] + (jnp.cumsum(grad_prefix[::-1], 0)[::-1] - grad_prefix)
    grad_v = grad_v + jnp.einsum("nshd,nhde->nshe", fk, grad_states, precision=HIGH)
    grad_fk = grad_fk + jnp.einsum("nshe,nhde->nshd", v_float, grad_states, precision=HIGH)
    query_grad = (grad_fq.reshape(tok, local_width) * feature_slope(q_float)).astype(jnp.bfloat16)
    key_grad = (grad_fk.reshape(tok, local_width) * feature_slope(k_float)).astype(jnp.bfloat16)
    value_grad = grad_v.reshape(tok, local_width).astype(jnp.bfloat16)
    return (layer_out, query_grad, key_grad, value_grad, weight_grad)


def solution(mesh):
    placed = (
        P(("rep", "ctx"), "head"),
        P(("rep", "ctx"), "head"),
        P(("rep", "ctx"), "head"),
        P("head", "ctx"),
        P(("rep", "ctx"), None),
    )
    return jax.shard_map(
        body,
        mesh=mesh,
        in_specs=placed,
        out_specs=(
            P(("rep", "ctx"), "head"),
            P(("rep", "ctx"), "head"),
            P(("rep", "ctx"), "head"),
            P(("rep", "ctx"), "head"),
            P(("rep", "head"), "ctx"),
        ),
        check_vma=False,
    )
```

profile of v0, /device:TPU:0, one launch (start us, length us, event | category | flops | bytes accessed | tf_op | source)
XLA Modules:
  0.0 131.6 jit_solution(13909327267743884201)
XLA Ops:
  7.2 0.0 copy-start.8
  7.2 0.0 all-gather.4.cloned.1.call-start
  7.2 0.7 all-gather.4.cloned.1.call-update
  7.9 0.0 reduce-scatter.5.cloned.1.call-start
  8.0 1.5 %fusion.18 = f32[512,512]{1,0:T(8,128)S(1)} fusion(bf16[512,512]{1,0:T(8,128)(2,1)} %param.10), kind=kLoop, calls=%fused_computation.41 | loop fusion | flops 1310720 | bytes 1572864 | tf_op jit(solution)/shard_map/add | solution.py:44
  9.5 0.4 reshape.82
  9.8 1.2 reshape.83
  11.0 0.0 copy-start
  11.0 0.0 copy-done.8
  11.0 0.4 fusion.15
  11.5 1.3 reshape.81
  12.8 1.5 %copy.69 = f32[4,128,4,128]{1,3,2,0:T(8,128)S(1)} copy(f32[4,128,4,128]{3,2,1,0:T(4,128)} %reshape.81) | data formatting | bytes 2097152 | tf_op jit(solution)/shard_map/reshape | solution.py:68
  14.3 2.0 %fusion.35 = (bf16[4,128,128]{2,1,0:T(8,128)(2,1)S(1)}, f32[4,4,128,128]{3,2,1,0:T(8,128)}) fusion(bf16[4,128,4,128]{3,2,1,0:T(4,128)(2,1)S(1)} %reshape.83, f32[4,128,4,128]{3,2,1,0:T(4,128)S(1)} %reshape.82), kind=kOutput, calls=%fused_computation.66 | convolution fusion | flops 402849792 | bytes 2752512 | tf_op jit(solution)/shard_map/nshd,nshe->nhde/dot_general | solution.py:71
  16.3 2.3 %all-gather = bf16[8,128,128]{2,1,0:T(8,128)(2,1)S(1)} all-gather(bf16[4,128,128]{2,1,0:T(8,128)(2,1)S(1)} %get-tuple-element.179), channel_id=2, replica_groups=mesh['ctx'=2,'head'=4,'rep'=4] {'ctx'}, dimensions={0}, use_global_device_ids=true | all-gather | bytes 393216 | tf_op jit(solution)/shard_map/all_gather | solution.py:16
  18.6 0.3 while.27
  18.6 0.1 add_select_fusion.2
  18.8 0.1 add_select_fusion.2
  18.9 3.0 %fusion.2 = f32[4,4,128,128]{3,2,1,0:T(8,128)} fusion(f32[4,4,128,128]{3,2,1,0:T(8,128)} %get-tuple-element.180, f32[4,128,128]{2,1,0:T(8,128)S(1)} %get-tuple-element.140), kind=kOutput, calls=%fused_computation.16 | output fusion | flops 1310720 | bytes 2359296 | tf_op jit(solution)/shard_map/jit(cumsum)/reduce_window_sum | solution.py:75
  21.9 1.8 %convolution_multiply_fusion.1 = f32[4,4,128,128]{3,2,1,0:T(8,128)S(1)} fusion(f32[4,128,4,128]{1,3,2,0:T(8,128)S(1)} %copy.69, f32[4,128,4,128]{3,2,1,0:T(4,128)S(1)} %reshape.82, f32[128,128]{1,0:T(8,128)S(1)} %fusion.33), kind=kOutput, calls=%fused_computation.25 | convolution fusion | flops 402915328 | bytes 3211264 | tf_op jit(solution)/shard_map/jvp(nthd,nshd->nhts)/dot_general | solution.py:54
  23.7 0.0 copy-done
  23.7 0.0 copy-start.4
  23.7 1.0 copy-done.4
  24.7 2.3 %convolution_bitcast_fusion.3 = f32[4,128,4,128]{1,3,2,0:T(8,128)} fusion(f32[4,4,128,128]{3,2,1,0:T(8,128)S(1)} %convolution_multiply_fusion.1, bf16[4,128,4,128]{3,2,1,0:T(4,128)(2,1)S(1)} %reshape.83), kind=kOutput, calls=%fused_computation.27 | convolution fusion | flops 402653184 | bytes 2621440 | tf_op jit(solution)/shard_map/jvp(nhts,nshe->nthe)/dot_general | solution.py:55
  27.0 6.8 %fusion.7 = f32[512,512]{1,0:T(8,128)} fusion(bf16[512,4096]{1,0:T(8,128)(2,1)} %param.13, bf16[512,4096]{1,0:T(8,128)(2,1)} %all-gather.4.cloned.1.call-done), kind=kOutput, calls=%fused_computation.30 | convolution fusion | flops 2148007936 | bytes 9437184 | tf_op jit(solution)/shard_map/dot_general | solution.py:87
  33.8 2.6 %reshape.91 = f32[4,128,4,128]{3,2,1,0:T(4,128)} reshape(f32[512,512]{1,0:T(8,128)} %fusion.7) | data formatting | bytes 2097152 | tf_op jit(solution)/shard_map/reshape | solution.py:99
  36.4 2.5 %copy.60 = f32[4,128,4,128]{1,3,2,0:T(8,128)} copy(f32[4,128,4,128]{3,2,1,0:T(4,128)} %reshape.91) | data formatting | bytes 2097152 | tf_op jit(solution)/shard_map/reshape | solution.py:99
  38.9 3.5 %multiply_reduce_fusion = (f32[4,128,4]{1,2,0:T(4,128)S(1)}, f32[4,128,4]{1,2,0:T(4,128)S(1)}, f32[4,128,4,128]{1,3,2,0:T(8,128)S(1)}) fusion(f32[4,128,4,128]{1,3,2,0:T(8,128)} %copy.60, f32[4,128,4,128]{1,3,2,0:T(8,128)} %convolution_bitcast_fusion.3, f32[4,4,128,128]{3,2,1,0:T(8,128)S(1)} %copy-done.2, f32[4,128,4,128]{1,3,2,0:T(8,128)S(1)} %copy.69), kind=kOutput, calls=%fused_computation.44 | convolution fusion | flops 403959808 | bytes 5259264 | tf_op jit(solution)/shard_map/jvp(nthd,nhde->nthe)/dot_general | solution.py:56
  42.5 1.1 fusion.9
  43.6 2.1 %copy.59 = bf16[4,128,4,128]{3,2,1,0:T(4,128)(2,1)} copy(bf16[4,128,4,128]{1,3,2,0:T(8,128)(2,1)} %get-tuple-element.176) | data formatting | bytes 1048576 | tf_op jit(solution)/shard_map/convert_element_type | solution.py:77
  45.7 6.7 %convolution_convert_fusion = bf16[512,4096]{1,0:T(8,128)(2,1)} fusion(bf16[512,4096]{1,0:T(8,128)(2,1)} %param.13, bf16[64,8,4,128]{3,2,1,0:T(4,128)(2,1)} %bitcast.76), kind=kOutput, calls=%fused_computation.2 | convolution fusion | flops 2149580800 | bytes 8912896 | tf_op jit(solution)/shard_map/dot_general | solution.py:93
  52.5 0.0 reduce-scatter.5.cloned.1.call-update
  52.5 0.3 reduce-scatter.3.cloned.1.call-start
  52.8 6.6 %convolution_convert_fusion.1 = bf16[512,4096]{1,0:T(8,128)(2,1)} fusion(bf16[512,4096]{1,0:T(8,128)(2,1)} %all-gather.4.cloned.1.call-done, bf16[64,8,4,128]{3,2,1,0:T(4,128)(2,1)} %bitcast.77), kind=kOutput, calls=%fused_computation.3 | convolution fusion | flops 2149580800 | bytes 8912896 | tf_op jit(solution)/shard_map/dot_general | solution.py:78
  59.4 0.0 reduce-scatter.3.cloned.1.call-update
  59.4 3.3 %fusion.36 = (bf16[4,128,128]{2,1,0:T(8,128)(2,1)S(1)}, f32[4,4,128,128]{3,2,1,0:T(8,128)}) fusion(f32[4,128,4,128]{1,3,2,0:T(8,128)S(1)} %copy.69, f32[4,4,128,128]{3,2,1,0:T(8,128)S(1)} %get-tuple-element.175), kind=kOutput, calls=%fused_computation.67 | convolution fusion | flops 402849792 | bytes 3276800 | tf_op jit(solution)/shard_map/transpose(jvp(nthd,nhde->nthe))/dot_general | solution.py:56
  62.7 2.6 %rev.6 = f32[4,4,128,128]{3,2,1,0:T(8,128)} reverse(f32[4,4,128,128]{3,2,1,0:T(8,128)} %get-tuple-element.183), dimensions={0} | reverse | bytes 2097152 | tf_op jit(solution)/shard_map/rev | solution.py:103
  65.3 2.1 %all-gather.1 = bf16[8,128,128]{2,1,0:T(8,128)(2,1)} all-gather(bf16[4,128,128]{2,1,0:T(8,128)(2,1)S(1)} %get-tuple-element.182), channel_id=3, replica_groups=mesh['ctx'=2,'head'=4,'rep'=4] {'ctx'}, dimensions={0}, use_global_device_ids=true | all-gather | bytes 393216 | tf_op jit(solution)/shard_map/all_gather | solution.py:31
  67.4 2.3 %fusion.37 = f32[4,4,128,128]{3,2,1,0:T(8,128)} fusion(f32[4,4,128,128]{3,2,1,0:T(8,128)} %rev.6), kind=kOutput, calls=%fused_computation.68 | output fusion | flops 786432 | bytes 2097152 | tf_op jit(solution)/shard_map/jit(cumsum)/reduce_window_sum | solution.py:103
  69.8 1.0 while.26
  69.8 1.0 convert_add_fusion.2
  70.8 1.7 %subtract_add_fusion = f32[4,4,128,128]{3,2,1,0:T(8,128)S(1)} fusion(f32[4,4,128,128]{3,2,1,0:T(8,128)} %get-tuple-element.183, f32[4,4,128,128]{3,2,1,0:T(8,128)} %fusion.37, f32[4,128,128]{2,1,0:T(8,128)S(1)} %get-tuple-element.141), kind=kLoop, calls=%fused_computation.43 | loop fusion | flops 524288 | bytes 3407872 | tf_op jit(solution)/shard_map/add | solution.py:103
  72.4 0.0 copy-start.6
  72.4 2.7 %fusion.39 = f32[4,4,128,128]{3,2,1,0:T(8,128)S(1)} fusion(f32[4,4,128,128]{3,2,1,0:T(8,128)S(1)} %get-tuple-element.175, f32[4,4,128,128]{3,2,1,0:T(8,128)} %copy-done.4), kind=kOutput, calls=%fused_computation.70 | convolution fusion | flops 402653184 | bytes 3145728 | tf_op jit(solution)/shard_map/transpose(jvp(nhts,nshe->nthe))/dot_general | solution.py:55
  75.2 2.7 %fusion.8 = bf16[4,128,4,128]{1,3,2,0:T(8,128)(2,1)} fusion(f32[4,4,128,128]{3,2,1,0:T(8,128)S(1)} %fusion.39, f32[4,4,128,128]{3,2,1,0:T(8,128)S(1)} %subtract_add_fusion, f32[4,128,4,128]{3,2,1,0:T(4,128)S(1)} %reshape.82), kind=kOutput, calls=%fused_computation.31 | convolution fusion | flops 403177472 | bytes 3670016 | tf_op jit(solution)/shard_map/nshd,nhde->nshe/dot_general | solution.py:104
  77.9 2.2 %copy.75 = bf16[4,128,4,128]{3,2,1,0:T(4,128)(2,1)} copy(bf16[4,128,4,128]{1,3,2,0:T(8,128)(2,1)} %fusion.8) | data formatting | bytes 1048576 | tf_op jit(solution)/shard_map/convert_element_type | solution.py:108
  80.1 2.0 %copy.117 = bf16[64,8,4,128]{3,1,2,0:T(8,128)(2,1)} copy(bf16[64,8,4,128]{3,2,1,0:T(4,128)(2,1)} %bitcast.78) | data formatting | bytes 1048576
  82.1 2.0 %convolution_multiply_fusion = f32[4,4,128,128]{3,2,1,0:T(8,128)S(1)} fusion(f32[4,4,128,128]{3,2,1,0:T(8,128)S(1)} %get-tuple-element.175, f32[128,128]{1,0:T(8,128)S(1)} %fusion.33, bf16[4,128,4,128]{3,2,1,0:T(4,128)(2,1)} %copy-done), kind=kOutput, calls=%fused_computation.22 | convolution fusion | flops 402915328 | bytes 2686976 | tf_op jit(solution)/shard_map/transpose(jvp(nhts,nshe->nthe))/dot_general | solution.py:55
  84.2 0.0 copy-start.1
  84.2 0.0 copy-start.7
  84.2 1.9 %fusion.38 = f32[4,4,128,128]{3,2,1,0:T(8,128)S(1)} fusion(f32[4,4,128,128]{3,2,1,0:T(8,128)S(1)} %get-tuple-element.175, f32[4,4,128,128]{3,2,1,0:T(8,128)S(1)} %copy-done.3), kind=kOutput, calls=%fused_computation.69 | convolution fusion | flops 402653184 | bytes 3145728 | tf_op jit(solution)/shard_map/transpose(jvp(nthd,nhde->nthe))/dot_general | solution.py:56
  86.0 1.2 fusion.4
  87.2 0.7 copy.66
  87.9 0.0 copy-done.1
  87.9 0.0 copy-done.7
  87.9 0.0 copy-start.9
  88.0 0.0 copy-start.10
  88.0 1.2 convolution_bitcast_fusion.2
  89.2 1.9 %fusion.3 = f32[4,128,4,128]{3,1,2,0:T(8,128)S(1)} fusion(f32[4,128,4,128]{3,1,2,0:T(8,128)S(1)} %convolution_bitcast_fusion.2, f32[4,4,128,128]{3,2,1,0:T(8,128)S(1)} %convolution_multiply_fusion, f32[4,128,4,128]{1,3,2,0:T(8,128)S(1)} %copy.69), kind=kOutput, calls=%fused_computation.19 | convolution fusion | flops 402915328 | bytes 4194304 | tf_op jit(solution)/shard_map/transpose(jvp(nthd,nshd->nhts))/dot_general | solution.py:54
  91.1 0.7 copy.72
  91.8 0.0 copy-done.9
  91.8 0.0 copy-done.10
  91.8 1.5 %fusion.11 = (bf16[512,512]{1,0:T(8,128)(2,1)}, bf16[512,512]{1,0:T(8,128)(2,1)}) fusion(bf16[512,512]{1,0:T(8,128)(2,1)S(1)} %copy-done.10, f32[64,8,4,128]{3,2,1,0:T(4,128)S(1)} %bitcast.73, bf16[512,512]{1,0:T(8,128)(2,1)S(1)} %copy-done.9, f32[64,8,4,128]{3,2,1,0:T(4,128)S(1)} %bitcast.72), kind=kLoop, calls=%fused_computation.34 | loop fusion | flops 3145728 | bytes 4194304 | tf_op jit(solution)/shard_map/convert_element_type | solution.py:107
  93.4 4.3 %convert_element_type.102 = f32[512,2048]{1,0:T(8,128)} convert(bf16[512,2048]{1,0:T(8,128)(2,1)} %reduce-scatter.5.cloned.1.call-done) | non-fusion elementwise | flops 1048576 | bytes 6291456 | tf_op jit(solution)/shard_map/convert_element_type | solution.py:98
  97.7 27.4 %reduce-scatter.3.cloned.1.call-done = bf16[512,1024]{1,0:T(8,128)(2,1)} async-done(((bf16[512,4096]{1,0:T(8,128)(2,1)}), bf16[512,1024]{1,0:T(8,128)(2,1)}) %reduce-scatter.3.cloned.1.call-update) | async-done | bytes 1048592 | tf_op jit(solution)/shard_map/reduce_scatter | solution.py:83
  (13 shorter events, 0.1 us)
Async XLA Ops:
  7.2 3.9 %copy-start.8 = (bf16[512,512]{1,0:T(8,128)(2,1)S(1)}, bf16[512,512]{1,0:T(8,128)(2,1)}, u32[]{:S(2)}) copy-start(bf16[512,512]{1,0:T(8,128)(2,1)} %param.9) | copy-start | bytes 1572868
  7.2 19.8 %all-gather.4.cloned.1.call-start = ((), (), s32[]{:S(2)}) async-start(), calls=%async_computation.2 | async-start | bytes 6291456 | tf_op jit(solution)/shard_map/all_gather | solution.py:80
  7.9 85.5 %reduce-scatter.5.cloned.1.call-start = ((), (), s32[]{:S(2)}) async-start(), calls=%async_computation.4 | async-start | bytes 6291456 | tf_op jit(solution)/shard_map/reduce_scatter | solution.py:96
  11.0 12.7 %copy-start = (bf16[4,128,4,128]{3,2,1,0:T(4,128)(2,1)}, bf16[4,128,4,128]{3,2,1,0:T(4,128)(2,1)S(1)}, u32[]{:S(2)}) copy-start(bf16[4,128,4,128]{3,2,1,0:T(4,128)(2,1)S(1)} %reshape.83) | copy-start | bytes 1572868
  23.7 1.0 copy-start.4
  33.8 5.2 %copy-start.2 = (f32[4,4,128,128]{3,2,1,0:T(8,128)S(1)}, f32[4,4,128,128]{3,2,1,0:T(8,128)}, u32[]{:S(2)}) copy-start(f32[4,4,128,128]{3,2,1,0:T(8,128)} %fusion.2) | copy-start | bytes 3145732
  38.9 3.6 %copy-start.5 = (f32[4,128,4,128]{1,3,2,0:T(8,128)S(1)}, f32[4,128,4,128]{1,3,2,0:T(8,128)}, u32[]{:S(2)}) copy-start(f32[4,128,4,128]{1,3,2,0:T(8,128)} %copy.60) | copy-start | bytes 3145732
  52.5 72.6 %reduce-scatter.3.cloned.1.call-start = ((), (), s32[]{:S(2)}) async-start(), calls=%async_computation.3 | async-start | bytes 5242880 | tf_op jit(solution)/shard_map/reduce_scatter | solution.py:83
  72.4 2.8 %copy-start.6 = (f32[4,4,128,128]{3,2,1,0:T(8,128)}, f32[4,4,128,128]{3,2,1,0:T(8,128)S(1)}, u32[]{:S(2)}) copy-start(f32[4,4,128,128]{3,2,1,0:T(8,128)S(1)} %subtract_add_fusion) | copy-start | bytes 3145732
  80.1 4.1 %copy-start.3 = (f32[4,4,128,128]{3,2,1,0:T(8,128)S(1)}, f32[4,4,128,128]{3,2,1,0:T(8,128)}, u32[]{:S(2)}) copy-start(f32[4,4,128,128]{3,2,1,0:T(8,128)} %fusion.2) | copy-start | bytes 3145732
  84.2 3.8 %copy-start.1 = (bf16[4,128,4,128]{3,2,1,0:T(4,128)(2,1)S(1)}, bf16[4,128,4,128]{3,2,1,0:T(4,128)(2,1)}, u32[]{:S(2)}) copy-start(bf16[4,128,4,128]{3,2,1,0:T(4,128)(2,1)} %copy-done) | copy-start | bytes 1572868
  84.2 3.8 %copy-start.7 = (f32[4,4,128,128]{3,2,1,0:T(8,128)S(1)}, f32[4,4,128,128]{3,2,1,0:T(8,128)}, u32[]{:S(2)}) copy-start(f32[4,4,128,128]{3,2,1,0:T(8,128)} %copy-done.6) | copy-start | bytes 3145732
  87.9 3.9 %copy-start.9 = (bf16[512,512]{1,0:T(8,128)(2,1)S(1)}, bf16[512,512]{1,0:T(8,128)(2,1)}, u32[]{:S(2)}) copy-start(bf16[512,512]{1,0:T(8,128)(2,1)} %param.9) | copy-start | bytes 1572868
  88.0 3.9 %copy-start.10 = (bf16[512,512]{1,0:T(8,128)(2,1)S(1)}, bf16[512,512]{1,0:T(8,128)(2,1)}, u32[]{:S(2)}) copy-start(bf16[512,512]{1,0:T(8,128)(2,1)} %param.10) | copy-start | bytes 1572868
Sparse Core Ops, SparseCore 0:
  9.6 16.3 all-gather.3
  52.6 14.6 reduce-scatter.4
  71.1 53.8 reduce-scatter.2
where the time goes:
time: 132 us
  matrix products  46.8 us (35%)
  waiting for transfers between devices  28.1 us (21%)
  local copies, waits for them, and re-layouts  20.8 us (16%)
  other arithmetic  17.1 us (13%)
  between operations  14 us (11%)
  blocking collectives  4.4 us (3%)
    reduce_scatter x1, waiting for transfers between devices, body(): lax.psum_scatter(partial_out.astype(jnp.bfloat16), 'head', scatter_dimens...  27.4 us
    dot_general x3, matrix products, tile_normed(): raw = raw + jnp.einsum('nthd,nhde->nthe', fq, prefix, precision=HIGH)  8.67 us
    dot_general x3, matrix products, tile_normed(): raw = jnp.einsum('nhts,nshe->nthe', scores, vals, precision=HIGH)  7.07 us
    dot_general x1, matrix products, body(): lax.dot_general(out_grad, lax.all_gather(out_weight, 'ctx', axis=1, tiled...  6.79 us
    dot_general x1, matrix products, body(): lax.dot_general(attn, out_grad, (((0,), (0,)), ((), ())), preferred_eleme...  6.75 us
    dot_general x1, matrix products, body(): jnp.dot(attn, lax.all_gather(out_weight, 'ctx', axis=1, tiled=True), pref...  6.65 us
    reshape x2, local copies, waits for them, and re-layouts, body(): cotangent = attn_grad.astype(jnp.float32).reshape(shape4)  5.15 us
    dot_general x3, matrix products, tile_normed(): scores = jnp.einsum('nthd,nshd->nhts', fq, fk, precision=HIGH) * lower  4.96 us
  transfers between devices with their start and end apart: 3, of which 1 were waited for; matrix products, arithmetic and copies ran while one was open for 44% of the time, Pallas kernels for 0%

commit v1 on v0

v1 whole, which is shorter than its diff:
```python
import functools

import jax
import jax.numpy as jnp
from jax import lax
from jax.experimental import pallas as pl
from jax.experimental.pallas import tpu as pltpu
from jax.sharding import PartitionSpec as P

DH = 128
CHUNK = 256
EPS = 1e-06
F32 = jnp.float32
BF16 = jnp.bfloat16


def feature(x):
    return jnp.where(x > 0, x + 1.0, jnp.exp(jnp.minimum(x, 0.0)))


def dot_nn(a, b):
    return lax.dot_general(a, b, (((1,), (0,)), ((), ())), preferred_element_type=F32)


def dot_nt(a, b):
    return lax.dot_general(a, b, (((1,), (1,)), ((), ())), preferred_element_type=F32)


def dot_tn(a, b):
    return lax.dot_general(a, b, (((0,), (0,)), ((), ())), preferred_element_type=F32)


def shape_of(shape, dtype):
    return jax.ShapeDtypeStruct(shape, dtype)


def params(mib):
    return pltpu.CompilerParams(vmem_limit_bytes=mib * 1024 * 1024)


def state_kernel(k_ref, v_ref, out_ref):
    for lo in range(0, k_ref.shape[1], DH):
        cols = slice(lo, lo + DH)
        fk = feature(k_ref[:, cols].astype(F32)).astype(BF16)
        out_ref[cols, :] = dot_tn(fk, v_ref[:, cols]).astype(BF16)


def local_state(keys, values):
    width = keys.shape[1]
    return pl.pallas_call(
        state_kernel, out_shape=shape_of((width, DH), BF16), compiler_params=params(32)
    )(keys, values)


def forward_kernel(q_ref, k_ref, v_ref, carried_ref, attn_ref, raw_ref, prefix_ref):
    tok, width = q_ref.shape
    chunk = min(CHUNK, tok)
    row = lax.broadcasted_iota(jnp.int32, (chunk, chunk), 0)
    col = lax.broadcasted_iota(jnp.int32, (chunk, chunk), 1)
    lower = row >= col
    for lo in range(0, width, DH):
        cols = slice(lo, lo + DH)
        prefix = carried_ref[cols, :].astype(F32)
        for i in range(tok // chunk):
            rows = slice(i * chunk, (i + 1) * chunk)
            fq = feature(q_ref[rows, cols].astype(F32)).astype(BF16)
            fk = feature(k_ref[rows, cols].astype(F32)).astype(BF16)
            v = v_ref[rows, cols]
            low_prefix = prefix.astype(BF16)
            prefix_ref[i, cols, :] = low_prefix
            scores = jnp.where(lower, dot_nt(fq, fk), 0.0).astype(BF16)
            raw = dot_nn(scores, v) + dot_nn(fq, low_prefix)
            raw_ref[rows, cols] = raw
            inv = lax.rsqrt(jnp.mean(raw * raw, axis=-1, keepdims=True) + EPS)
            attn_ref[rows, cols] = (raw * inv).astype(BF16)
            if i + 1 < tok // chunk:
                prefix = prefix + dot_tn(fk, v)


def forward(queries, keys, values, carried):
    tok, width = queries.shape
    chunks = tok // min(CHUNK, tok)
    return pl.pallas_call(
        forward_kernel,
        out_shape=(
            shape_of((tok, width), BF16),
            shape_of((tok, width), F32),
            shape_of((chunks, width, DH), BF16),
        ),
        compiler_params=params(32),
    )(queries, keys, values, carried)


def cotangent_kernel(own_blocks, s_ref, grad_ref, own_ref, rest_ref, q_ref, raw_ref,
                     draw_ref, gsum_ref, glocal_ref, acc_ref):
    step = pl.program_id(0)

    @pl.when(step == 0)
    def _():
        acc_ref[...] = dot_nt(grad_ref[...], own_ref[...])

    @pl.when((step > 0) & (step < own_blocks))
    def _():
        acc_ref[...] += dot_nt(grad_ref[...], own_ref[...])

    @pl.when(step >= own_blocks)
    def _():
        acc_ref[...] += dot_nt(grad_ref[...], rest_ref[...])

    @pl.when(step == pl.num_programs(0) - 1)
    def _():
        tok, width = q_ref.shape
        chunk = min(CHUNK, tok)
        for lo in range(0, width, DH):
            cols = slice(lo, lo + DH)
            later = jnp.zeros((DH, DH), F32)
            for i in reversed(range(tok // chunk)):
                rows = slice(i * chunk, (i + 1) * chunk)
                glocal_ref[i, cols, :] = later
                grad = acc_ref[rows, cols].astype(BF16).astype(F32)
                raw = raw_ref[rows, cols]
                inv = lax.rsqrt(jnp.mean(raw * raw, axis=-1, keepdims=True) + EPS)
                normed = raw * inv
                mean = jnp.mean(grad * normed, axis=-1, keepdims=True)
                draw = (inv * (grad - normed * mean)).astype(BF16)
                draw_ref[rows, cols] = draw
                fq = feature(q_ref[rows, cols].astype(F32)).astype(BF16)
                later = later + dot_tn(fq, draw)
            gsum_ref[cols, :] = later.astype(BF16)


def cotangent(scal, out_grad, own, rest, queries, raw):
    tok, width = queries.shape
    block = min(1024, own.shape[1])
    own_blocks = own.shape[1] // block
    blocks = out_grad.shape[1] // block
    chunks = tok // min(CHUNK, tok)
    whole = lambda *dims: pl.BlockSpec(dims, lambda j, s: (0,) * len(dims))
    return pl.pallas_call(
        functools.partial(cotangent_kernel, own_blocks),
        out_shape=(
            shape_of((tok, width), BF16),
            shape_of((width, DH), BF16),
            shape_of((chunks, width, DH), F32),
        ),
        grid_spec=pltpu.PrefetchScalarGridSpec(
            num_scalar_prefetch=1,
            grid=(blocks,),
            in_specs=[
                pl.BlockSpec((tok, block), lambda j, s: (0, lax.rem(s[0] * own_blocks + j, blocks))),
                pl.BlockSpec((width, block), lambda j, s: (0, jnp.minimum(j, own_blocks - 1))),
                pl.BlockSpec((width, block), lambda j, s: (0, jnp.maximum(j - own_blocks, 0))),
                whole(tok, width),
                whole(tok, width),
            ],
            out_specs=(whole(tok, width), whole(width, DH), whole(chunks, width, DH)),
            scratch_shapes=[pltpu.VMEM((tok, width), F32)],
        ),
        compiler_params=params(40),
    )(scal, out_grad, own, rest, queries, raw)


def term_kernel(s_ref, attn_ref, grad_ref, out_ref):
    out_ref[...] = dot_tn(attn_ref[...], grad_ref[...]).astype(BF16)


def term_for_others(scal, attn, out_grad, own_width):
    tok, width = attn.shape
    block = min(1024, own_width)
    own_blocks = own_width // block
    blocks = out_grad.shape[1] // block
    return pl.pallas_call(
        term_kernel,
        out_shape=shape_of((width, out_grad.shape[1] - own_width), BF16),
        grid_spec=pltpu.PrefetchScalarGridSpec(
            num_scalar_prefetch=1,
            grid=(blocks - own_blocks,),
            in_specs=[
                pl.BlockSpec((tok, width), lambda j, s: (0, 0)),
                pl.BlockSpec(
                    (tok, block), lambda j, s: (0, lax.rem(s[0] * own_blocks + own_blocks + j, blocks))
                ),
            ],
            out_specs=pl.BlockSpec((width, block), lambda j, s: (0, j)),
        ),
        compiler_params=params(32),
    )(scal, attn, out_grad)


def weight_grad_kernel(s_ref, attn_ref, grad_ref, others_ref, out_ref):
    term = dot_tn(attn_ref[...], grad_ref[...]).astype(BF16)
    out_ref[...] = term.astype(F32) + others_ref[...].astype(F32)


def own_weight_grad(scal, attn, out_grad, others):
    tok, width = attn.shape
    own_width = others.shape[1]
    block = min(1024, own_width)
    own_blocks = own_width // block
    return pl.pallas_call(
        weight_grad_kernel,
        out_shape=shape_of((width, own_width), F32),
        grid_spec=pltpu.PrefetchScalarGridSpec(
            num_scalar_prefetch=1,
            grid=(own_blocks,),
            in_specs=[
                pl.BlockSpec((tok, width), lambda j, s: (0, 0)),
                pl.BlockSpec((tok, block), lambda j, s: (0, s[0] * own_blocks + j)),
                pl.BlockSpec((width, block), lambda j, s: (0, j)),
            ],
            out_specs=pl.BlockSpec((width, block), lambda j, s: (0, j)),
        ),
        compiler_params=params(32),
    )(scal, attn, out_grad, others)


def backward_kernel(q_ref, k_ref, v_ref, draw_ref, prefix_ref, suffix_ref, glocal_ref,
                    dq_ref, dk_ref, dv_ref):
    tok, width = q_ref.shape
    chunk = min(CHUNK, tok)
    row = lax.broadcasted_iota(jnp.int32, (chunk, chunk), 0)
    col = lax.broadcasted_iota(jnp.int32, (chunk, chunk), 1)
    lower = row >= col
    upper = row <= col
    for lo in range(0, width, DH):
        cols = slice(lo, lo + DH)
        suffix = suffix_ref[cols, :].astype(F32)
        for i in range(tok // chunk):
            rows = slice(i * chunk, (i + 1) * chunk)
            q = q_ref[rows, cols].astype(F32)
            k = k_ref[rows, cols].astype(F32)
            q_slope = jnp.exp(jnp.minimum(q, 0.0))
            k_slope = jnp.exp(jnp.minimum(k, 0.0))
            fq = jnp.where(q > 0, q + 1.0, q_slope).astype(BF16)
            fk = jnp.where(k > 0, k + 1.0, k_slope).astype(BF16)
            v = v_ref[rows, cols]
            draw = draw_ref[rows, cols]
            later = (suffix + glocal_ref[i, cols, :]).astype(BF16)
            dscores = jnp.where(lower, dot_nt(draw, v), 0.0).astype(BF16)
            dfq = dot_nn(dscores, fk) + dot_nt(draw, prefix_ref[i, cols, :])
            dq_ref[rows, cols] = (dfq * q_slope).astype(BF16)
            dscores_t = jnp.where(upper, dot_nt(v, draw), 0.0).astype(BF16)
            dfk = dot_nn(dscores_t, fq) + dot_nt(v, later)
            dk_ref[rows, cols] = (dfk * k_slope).astype(BF16)
            scores_t = jnp.where(upper, dot_nt(fk, fq), 0.0).astype(BF16)
            dv = dot_nn(scores_t, draw) + dot_nn(fk, later)
            dv_ref[rows, cols] = dv.astype(BF16)


def backward(queries, keys, values, draw, prefix, suffix, glocal):
    out = shape_of(queries.shape, BF16)
    return pl.pallas_call(
        backward_kernel, out_shape=(out, out, out), compiler_params=params(40)
    )(queries, keys, values, draw, prefix, suffix, glocal)


def project_kernel(s_ref, a_ref, a1_ref, a2_ref, a3_ref, own_ref, rest_ref,
                   m1_ref, z1_ref, o1_ref, oz1_ref, d_ref, dz_ref, od_ref, odz_ref, out_ref, acc_ref):
    half = m1_ref.shape[0]
    first = pl.ds(pl.multiple_of(s_ref[3] * half, half), half)
    second = pl.ds(pl.multiple_of((1 - s_ref[3]) * half, half), half)

    @pl.when(s_ref[0] == s_ref[1])
    def _():
        acc_ref[...] = dot_nn(a_ref[...], own_ref[...])

    @pl.when(s_ref[0] != s_ref[1])
    def _():
        acc_ref[...] = dot_nn(a_ref[...], rest_ref[...])

    acc = acc_ref[...]
    acc += dot_nn(a1_ref[:, first], m1_ref[...])
    acc += dot_nn(a1_ref[:, second], z1_ref[...])
    acc += dot_nn(a2_ref[:, first], o1_ref[...])
    acc += dot_nn(a2_ref[:, second], oz1_ref[...])
    acc += dot_nn(a3_ref[:, first], d_ref[...] + od_ref[...])
    acc += dot_nn(a3_ref[:, second], dz_ref[...] + odz_ref[...])
    out_ref[...] = acc.astype(BF16)


def project(scal, attns, own, rest, pieces):
    tok, width = attns[0].shape
    half, out_width = pieces[0].shape
    block = 512
    blocks = out_width // block
    whole = pl.BlockSpec((tok, width), lambda j, s: (0, 0))
    local = pl.BlockSpec((width, block), lambda j, s: (0, s[2] * blocks + j))
    piece = pl.BlockSpec((half, block), lambda j, s: (0, j))
    return pl.pallas_call(
        project_kernel,
        out_shape=shape_of((tok, out_width), BF16),
        grid_spec=pltpu.PrefetchScalarGridSpec(
            num_scalar_prefetch=1,
            grid=(blocks,),
            in_specs=[whole] * 4 + [local] * 2 + [piece] * 8,
            out_specs=pl.BlockSpec((tok, block), lambda j, s: (0, j)),
            scratch_shapes=[pltpu.VMEM((tok, block), F32)],
        ),
        compiler_params=params(40),
    )(scal, *attns, own, rest, *pieces)


def shift(array, axis, count, by, wrap):
    pairs = [(i, (i + by) % count) for i in range(count) if wrap or 0 <= i + by < count]
    return lax.ppermute(array, axis, pairs)


def total(arrays):
    if len(arrays) == 1:
        return arrays[0]
    return functools.reduce(jnp.add, [a.astype(F32) for a in arrays])


def body(n_ctx, n_head, n_rep, queries, keys, values, out_weight, out_grad):
    c, h, z = lax.axis_index("ctx"), lax.axis_index("head"), lax.axis_index("rep")
    x, y, p = h % 2, h // 2, z % 2
    scal = jnp.stack([c, y, x, p]).astype(jnp.int32)
    paired = n_ctx == 2 and n_head == 4 and n_rep % 2 == 0
    own_width = out_weight.shape[1]

    if paired:
        group = ("ctx", "head")
        half, wide = out_weight.shape[0] // 2, out_weight.shape[1] // 2
        near = [(4 * (i // 2) + i, i ^ 1) for i in range(4)]
        near += [(4 * (1 - i // 2) + i, 4 + (i ^ 2)) for i in range(4)]
        far = [(4 * (1 - i // 2) + i, i ^ 3) for i in range(4)]
        start = p * half
        near_piece = lax.dynamic_slice(
            out_weight, (start, wide * jnp.where(c == y, 1 - x, x)), (half, wide)
        )
        far_piece = lax.dynamic_slice(out_weight, (start, wide * (1 - x)), (half, wide))
        near_mine = lax.ppermute(near_piece, group, near)
        far_mine = lax.ppermute(far_piece, group, far)

    rest = [shift(out_weight, "ctx", n_ctx, -k, True) for k in range(1, n_ctx)]
    rest = rest[0] if n_ctx == 2 else jnp.concatenate(rest, 1)

    state = local_state(keys, values)
    carried = total([shift(state, "ctx", n_ctx, k, False) for k in range(1, n_ctx)])
    attn, raw, prefix = forward(queries, keys, values, carried)

    if paired:
        zpair = [(i, i ^ 1) for i in range(n_rep)]
        swap = [(0, 1), (1, 0)]
        one = [(i, i ^ 1) for i in range(4)] + [(4 + i, 4 + (i ^ 2)) for i in range(4)]
        two = [(i, i ^ 2) for i in range(4)] + [(4 + i, 4 + (i ^ 1)) for i in range(4)]
        attn_1 = lax.ppermute(attn, group, one)
        attn_2 = lax.ppermute(attn, group, two)
        near_z = lax.ppermute(near_mine, "rep", zpair)
        far_z = lax.ppermute(far_mine, "rep", zpair)
        attn_3 = lax.ppermute(attn_1, group, two)
        near_other = lax.ppermute(near_mine, "ctx", swap)
        near_other_z = lax.ppermute(near_z, "ctx", swap)
        far_other = lax.ppermute(far_mine, "ctx", swap)
        far_other_z = lax.ppermute(far_z, "ctx", swap)

    draw, gsum, glocal = cotangent(scal, out_grad, out_weight, rest, queries, raw)
    suffix = total([shift(gsum, "ctx", n_ctx, -k, False) for k in range(1, n_ctx)])

    terms = term_for_others(scal, attn, out_grad, own_width)
    others = []
    for k in range(1, n_ctx):
        term = terms[:, (k - 1) * own_width : k * own_width] if n_ctx > 2 else terms
        others.append(shift(term, "ctx", n_ctx, k, True))
    query_grad, key_grad, value_grad = backward(queries, keys, values, draw, prefix, suffix, glocal)
    weight_grad = own_weight_grad(scal, attn, out_grad, total(others))

    if paired:
        layer_out = project(
            scal, (attn, attn_1, attn_2, attn_3), out_weight, rest,
            (near_mine, near_z, near_other, near_other_z, far_mine, far_z, far_other, far_other_z),
        )
    else:
        full = lax.all_gather(out_weight, "ctx", axis=1, tiled=True)
        partial_out = jnp.dot(attn, full, preferred_element_type=F32).astype(BF16)
        layer_out = lax.psum_scatter(partial_out, "head", scatter_dimension=1, tiled=True)
    return layer_out, query_grad, key_grad, value_grad, weight_grad


def solution(mesh):
    tokens = P(("rep", "ctx"), "head")
    sizes = mesh.shape["ctx"], mesh.shape["head"], mesh.shape["rep"]
    return jax.shard_map(
        functools.partial(body, *sizes),
        mesh=mesh,
        in_specs=(tokens, tokens, tokens, P("head", "ctx"), P(("rep", "ctx"), None)),
        out_specs=(tokens, tokens, tokens, tokens, P(("rep", "head"), "ctx")),
        check_vma=False,
    )
```

time: 132 us -> 76.9 us (0.58)
  matrix products: 46.8 us -> 0 us
  Pallas kernels: 0 us -> 22.4 us
  starting transfers between devices: 0.34 us -> 21.1 us
  other arithmetic: 17.1 us -> 0.08 us
  local copies, waits for them, and re-layouts: 20.8 us -> 5.62 us
  between operations: 14 us -> 0.83 us
  blocking collectives: 4.4 us -> 0 us
  waiting for transfers between devices: 28.1 us -> 25.9 us
    dot_general x15 -> x0, matrix products: 46.8 us -> none  [the longest x3 8.67 us: tile_normed(): raw = raw + jnp.einsum('nthd,nhde->nthe', fq, prefix, precision=HIGH)]
    reduce_scatter x2 -> x0, waiting for transfers between devices: 27.4 us -> none  [the longest x1 27.4 us: body(): lax.psum_scatter(partial_out.astype(jnp.bfloat16), 'head', scatter_dimens...]
    ppermute x0 -> x15, waiting for transfers between devices: none -> 25.9 us  [the longest x1 11.1 us: body(): far_mine = lax.ppermute(far_piece, group, far)]
    pallas_call x0 -> x7, Pallas kernels: none -> 22.4 us  [the longest x1 5.7 us: cotangent(): pl.pallas_call(functools.partial(cotangent_kernel, own_blocks), out_shape...]
    ppermute x0 -> x15, starting transfers between devices: none -> 21.1 us  [the longest x1 4.99 us: body(): near_other = lax.ppermute(near_mine, 'ctx', swap)]
    reshape x6 -> x0, local copies, waits for them, and re-layouts: 9.53 us -> none  [the longest x2 5.15 us: body(): cotangent = attn_grad.astype(jnp.float32).reshape(shape4)]
    convert_element_type x2 -> x0, other arithmetic: 5.84 us -> none  [the longest x1 4.32 us: body(): weight_grad = lax.psum_scatter(term.astype(jnp.bfloat16), 'ctx', scatter_...]
    another operation x2 -> x1, other arithmetic: 5.3 us -> 0.08 us  [body(): scal = jnp.stack([c, y, x, p]).astype(jnp.int32)]
  transfers between devices with their start and end apart: 3 -> 15, of which waited for: 1 -> 3; matrix products, arithmetic and copies ran while one was open for 44% -> 2% of each run, Pallas kernels for 0% -> 25%
where the time goes in v1:
time: 76.9 us; the launch traced here: 75.9 us
  waiting for transfers between devices  25.9 us (34%)
  Pallas kernels  22.4 us (29%)
  starting transfers between devices  21.1 us (27%)
  local copies, waits for them, and re-layouts  5.62 us (7%)
  between operations  0.83 us (1%)
    ppermute x1, waiting for transfers between devices, body(): far_mine = lax.ppermute(far_piece, group, far)  11.1 us
    ppermute x1, waiting for transfers between devices, body(): far_z = lax.ppermute(far_mine, 'rep', zpair)  8.76 us
    ppermute x1, waiting for transfers between devices, body(): near_z = lax.ppermute(near_mine, 'rep', zpair)  5.96 us
    pallas_call x1, Pallas kernels, cotangent(): pl.pallas_call(functools.partial(cotangent_kernel, own_blocks), out_shape...  5.7 us
    ppermute x1, starting transfers between devices, body(): near_other = lax.ppermute(near_mine, 'ctx', swap)  4.99 us
    pallas_call x1, Pallas kernels, project(): pl.pallas_call(project_kernel, out_shape=shape_of((tok, out_width), BF16)...  4.78 us
    unnamed x16, local copies, waits for them, and re-layouts  4.29 us
    ppermute x4, starting transfers between devices, shift(): return lax.ppermute(array, axis, pairs)  4.06 us
  transfers between devices with their start and end apart: 15, of which 3 were waited for; matrix products, arithmetic and copies ran while one was open for 2% of the time, Pallas kernels for 25%

profile of v1, /device:TPU:0, one launch (start us, length us, event | category | flops | bytes accessed | tf_op | source)
XLA Modules:
  0.0 75.9 jit_solution(8581124488675229609)
XLA Ops:
  0.6 0.0 copy-start.3
  0.6 0.5 collective-permute-start.4
  1.2 0.0 copy-start.4
  1.2 1.0 %copy-done.4 = bf16[512,512]{1,0:T(8,128)(2,1)S(1)} copy-done((bf16[512,512]{1,0:T(8,128)(2,1)S(1)}, bf16[512,512]{1,0:T(8,128)(2,1)}, u32[]{:S(2)}) %copy-start.4) | copy-done | bytes 524312
  2.2 0.0 copy-start.6
  2.2 1.0 %copy-done.6 = bf16[512,512]{1,0:T(8,128)(2,1)S(1)} copy-done((bf16[512,512]{1,0:T(8,128)(2,1)S(1)}, bf16[512,512]{1,0:T(8,128)(2,1)}, u32[]{:S(2)}) %copy-start.6) | copy-done | bytes 524312
  3.2 0.0 copy-start.5
  3.2 0.5 shard_map.92
  3.8 2.0 %collective-permute-start = (bf16[512,128]{1,0:T(8,128)(2,1)S(1)}, bf16[512,128]{1,0:T(8,128)(2,1)S(1)}, u32[]{:S(2)}, u32[]{:S(2)}) collective-permute-start(bf16[512,128]{1,0:T(8,128)(2,1)S(1)} %shard_map.92), channel_id=1, source_target_pairs={{0,16},{1,17},{2,18},{3,19},{4,20},{5,21},{6,22},{7,23},{8,24},{9,... | collective-permute-start | bytes 393224 | tf_op jit(solution)/shard_map/ppermute | solution.py:305
  5.8 0.0 copy-start.7
  5.8 1.3 %fusion = (bf16[256,1024]{1,0:T(8,128)(2,1)S(1)}, bf16[256,1024]{1,0:T(8,128)(2,1)S(1)}) fusion(bf16[512,2048]{1,0:T(8,128)(2,1)} %own_ref.3, s32[]{:T(128)S(6)} %select_n.31, s32[]{:T(128)S(6)} %select_n.34, s32[]{:T(128)S(6)} %select_n.33), kind=kLoop, calls=%fused_computation.1 | loop fusion | bytes 2097164 | tf_op jit(solution)/shard_map/dynamic_slice | solution.py:331
  7.2 3.0 %collective-permute-start.5 = (bf16[256,1024]{1,0:T(8,128)(2,1)S(1)}, bf16[256,1024]{1,0:T(8,128)(2,1)S(1)}, u32[]{:S(2)}, u32[]{:S(2)}) collective-permute-start(bf16[256,1024]{1,0:T(8,128)(2,1)S(1)} %get-tuple-element.24), channel_id=1, source_target_pairs={{0,4},{4,0},{24,12},{28,8},{16,24},{20,28},{8,16},{12,20},{1,5},{5... | collective-permute-start | bytes 1572872 | tf_op jit(solution)/shard_map/ppermute | solution.py:332
  10.1 0.1 pad_add_fusion.s_ref
  10.2 0.0 collective-permute-done.carried_ref
  10.2 0.0 copy-done.3
  10.2 0.0 copy-done.5
  10.2 0.0 copy-done.7
  10.2 1.5 %shard_map.93 = (bf16[512,512]{1,0:T(8,128)(2,1)S(1)}, f32[512,512]{1,0:T(8,128)S(1)}, bf16[2,512,128]{2,1,0:T(8,128)(2,1)S(1)}) custom-call(bf16[512,512]{1,0:T(8,128)(2,1)S(1)} %copy-done.3, bf16[512,512]{1,0:T(8,128)(2,1)S(1)} %copy-done.5, bf16[512,512]{1,0:T(8,128)(2,1)S(1)} %copy-done.7, bf16[512,128]{1,0:T(8,128)(2,1)S(1)} %collective-permute-done.carried_ref), custom_call_target="tpu_custom_call" | custom-call | tf_op jit(solution)/shard_map/pallas_call | solution.py:83
  11.8 0.0 copy-start
  11.8 2.2 %copy-done = bf16[512,4096]{1,0:T(8,128)(2,1)S(1)} copy-done((bf16[512,4096]{1,0:T(8,128)(2,1)S(1)}, bf16[512,4096]{1,0:T(8,128)(2,1)}, u32[]{:S(2)}) %copy-start) | copy-done | bytes 4194328
  14.0 0.0 copy-start.1
  14.0 0.0 copy-start.2
  14.0 2.4 %shard_map.97 = bf16[512,2048]{1,0:T(8,128)(2,1)S(1)} custom-call(s32[4]{0:T(128)S(1)} %pad_add_fusion.s_ref, bf16[512,512]{1,0:T(8,128)(2,1)S(1)} %get-tuple-element.14.a_ref.attn_ref, bf16[512,4096]{1,0:T(8,128)(2,1)S(1)} %copy-done), custom_call_target="tpu_custom_call" | custom-call | tf_op jit(solution)/shard_map/pallas_call | solution.py:172
  16.4 0.1 collective-permute-start.14
  16.4 1.3 %collective-permute-start.9 = (bf16[256,1024]{1,0:T(8,128)(2,1)S(1)}, bf16[256,1024]{1,0:T(8,128)(2,1)S(1)}, u32[]{:S(2)}, u32[]{:S(2)}) collective-permute-start(bf16[256,1024]{1,0:T(8,128)(2,1)S(1)} %get-tuple-element.23), channel_id=1, source_target_pairs={{16,12},{20,8},{8,4},{12,0},{17,13},{21,9},{9,5},{13,1},{18,14},{2... | collective-permute-start | bytes 1572872 | tf_op jit(solution)/shard_map/ppermute | solution.py:333
  17.7 0.7 collective-permute-start.1
  18.4 0.0 collective-permute-done.5.m1_ref
  18.4 3.5 %collective-permute-start.2 = (bf16[512,512]{1,0:T(8,128)(2,1)S(1)}, bf16[512,512]{1,0:T(8,128)(2,1)S(1)}, u32[]{:S(2)}, u32[]{:S(2)}) collective-permute-start(bf16[512,512]{1,0:T(8,128)(2,1)S(1)} %get-tuple-element.14.a_ref.attn_ref), channel_id=1, source_target_pairs={{0,8},{4,12},{8,0},{12,4},{16,20},{20,16},{24,28},{28,24},{1,9},{5... | collective-permute-start | bytes 1572872 | tf_op jit(solution)/shard_map/ppermute | solution.py:348
  21.9 11.1 %collective-permute-done.9.d_ref = bf16[256,1024]{1,0:T(8,128)(2,1)S(1)} collective-permute-done((bf16[256,1024]{1,0:T(8,128)(2,1)S(1)}, bf16[256,1024]{1,0:T(8,128)(2,1)S(1)}, u32[]{:S(2)}, u32[]{:S(2)}) %collective-permute-start.9) | collective-permute-done | bytes 524320 | tf_op jit(solution)/shard_map/ppermute | solution.py:333
  33.0 1.6 %collective-permute-start.6 = (bf16[256,1024]{1,0:T(8,128)(2,1)S(1)}, bf16[256,1024]{1,0:T(8,128)(2,1)S(1)}, u32[]{:S(2)}, u32[]{:S(2)}) collective-permute-start(bf16[256,1024]{1,0:T(8,128)(2,1)S(1)} %collective-permute-done.5.m1_ref), channel_id=1, source_target_pairs={{0,1},{1,0},{2,3},{3,2},{4,5},{5,4},{6,7},{7,6},{8,9},{9,8},{10,11... | collective-permute-start | bytes 1572872 | tf_op jit(solution)/shard_map/ppermute | solution.py:349
  34.6 0.0 collective-permute-done.1.a1_ref
  34.6 5.0 %collective-permute-start.7 = (bf16[256,1024]{1,0:T(8,128)(2,1)S(1)}, bf16[256,1024]{1,0:T(8,128)(2,1)S(1)}, u32[]{:S(2)}, u32[]{:S(2)}) collective-permute-start(bf16[256,1024]{1,0:T(8,128)(2,1)S(1)} %collective-permute-done.5.m1_ref), channel_id=1, source_target_pairs={{0,16},{16,0},{1,17},{17,1},{2,18},{18,2},{3,19},{19,3},{4,20},{20... | collective-permute-start | bytes 1572872 | tf_op jit(solution)/shard_map/ppermute | solution.py:352
  39.5 0.0 collective-permute-done.2.a2_ref
  39.6 1.6 %collective-permute-start.10 = (bf16[256,1024]{1,0:T(8,128)(2,1)S(1)}, bf16[256,1024]{1,0:T(8,128)(2,1)S(1)}, u32[]{:S(2)}, u32[]{:S(2)}) collective-permute-start(bf16[256,1024]{1,0:T(8,128)(2,1)S(1)} %collective-permute-done.9.d_ref), channel_id=1, source_target_pairs={{0,1},{1,0},{2,3},{3,2},{4,5},{5,4},{6,7},{7,6},{8,9},{9,8},{10,11... | collective-permute-start | bytes 1572872 | tf_op jit(solution)/shard_map/ppermute | solution.py:350
  41.2 6.0 %collective-permute-done.6.z1_ref = bf16[256,1024]{1,0:T(8,128)(2,1)S(1)} collective-permute-done((bf16[256,1024]{1,0:T(8,128)(2,1)S(1)}, bf16[256,1024]{1,0:T(8,128)(2,1)S(1)}, u32[]{:S(2)}, u32[]{:S(2)}) %collective-permute-start.6) | collective-permute-done | bytes 524320 | tf_op jit(solution)/shard_map/ppermute | solution.py:349
  47.1 0.0 collective-permute-start.11
  47.1 0.0 collective-permute-done.7.o1_ref
  47.1 0.0 collective-permute-start.3
  47.1 8.8 %collective-permute-done.10.dz_ref = bf16[256,1024]{1,0:T(8,128)(2,1)S(1)} collective-permute-done((bf16[256,1024]{1,0:T(8,128)(2,1)S(1)}, bf16[256,1024]{1,0:T(8,128)(2,1)S(1)}, u32[]{:S(2)}, u32[]{:S(2)}) %collective-permute-start.10) | collective-permute-done | bytes 524320 | tf_op jit(solution)/shard_map/ppermute | solution.py:350
  55.9 0.0 collective-permute-start.8
  55.9 0.0 collective-permute-done.4.rest_ref
  55.9 0.5 collective-permute-start.12
  56.4 0.0 copy-done.1
  56.4 0.0 copy-done.2
  56.4 5.7 %shard_map.95 = (bf16[512,512]{1,0:T(8,128)(2,1)S(1)}, bf16[512,128]{1,0:T(8,128)(2,1)S(1)}, f32[2,512,128]{2,1,0:T(8,128)S(1)}) custom-call(s32[4]{0:T(128)S(1)} %pad_add_fusion.s_ref, bf16[512,4096]{1,0:T(8,128)(2,1)S(1)} %copy-done.1, bf16[512,2048]{1,0:T(8,128)(2,1)S(1)} %copy-done.2, bf16[512,2048]{1,0:T(8,128)(2,1)S(1)} %collective-permute-done.4.rest_ref, ...), custom_call_target="tpu_custom_call" | custom-call | tf_op jit(solution)/shard_map/pallas_call | solution.py:139
  62.1 0.0 collective-permute-done.11.od_ref
  62.1 1.5 %collective-permute-start.13 = (bf16[512,128]{1,0:T(8,128)(2,1)S(1)}, bf16[512,128]{1,0:T(8,128)(2,1)S(1)}, u32[]{:S(2)}, u32[]{:S(2)}) collective-permute-start(bf16[512,128]{1,0:T(8,128)(2,1)S(1)} %get-tuple-element.18), channel_id=1, source_target_pairs={{16,0},{17,1},{18,2},{19,3},{20,4},{21,5},{22,6},{23,7},{24,8},{25... | collective-permute-start | bytes 393224 | tf_op jit(solution)/shard_map/ppermute | solution.py:305
  63.6 0.0 collective-permute-done.3.a3_ref
  63.6 0.0 collective-permute-done.8.oz1_ref
  63.6 0.0 collective-permute-done.12.odz_ref
  63.7 4.8 %shard_map.94 = bf16[512,1024]{1,0:T(8,128)(2,1)} custom-call(s32[4]{0:T(128)S(1)} %pad_add_fusion.s_ref, bf16[512,512]{1,0:T(8,128)(2,1)S(1)} %get-tuple-element.14.a_ref.attn_ref, bf16[512,512]{1,0:T(8,128)(2,1)S(1)} %collective-permute-done.1.a1_ref, bf16[512,512]{1,0:T(8,128)(2,1)S(1)} %collective-permute-done.2.a2_ref, ...), custom_call_target="tpu_custom_call" | custom-call | tf_op jit(solution)/shard_map/pallas_call | solution.py:289
  68.4 0.0 collective-permute-done.14.others_ref
  68.4 3.7 %shard_map.98 = f32[512,2048]{1,0:T(8,128)} custom-call(s32[4]{0:T(128)S(1)} %pad_add_fusion.s_ref, bf16[512,512]{1,0:T(8,128)(2,1)S(1)} %get-tuple-element.14.a_ref.attn_ref, bf16[512,4096]{1,0:T(8,128)(2,1)S(1)} %copy-done.1, bf16[512,2048]{1,0:T(8,128)(2,1)S(1)} %collective-permute-done.14.others_ref), custom_call_target="tpu_custom_call" | custom-call | tf_op jit(solution)/shard_map/pallas_call | solution.py:200
  72.2 0.0 collective-permute-done.13.suffix_ref
  72.2 3.8 %shard_map.96 = (bf16[512,512]{1,0:T(8,128)(2,1)}, bf16[512,512]{1,0:T(8,128)(2,1)}, bf16[512,512]{1,0:T(8,128)(2,1)}) custom-call(bf16[512,512]{1,0:T(8,128)(2,1)S(1)} %copy-done.3, bf16[512,512]{1,0:T(8,128)(2,1)S(1)} %copy-done.5, bf16[512,512]{1,0:T(8,128)(2,1)S(1)} %copy-done.7, bf16[512,512]{1,0:T(8,128)(2,1)S(1)} %get-tuple-element.16.draw_ref, ...), custom_call_target="tpu_custom_call" | custom-call | tf_op jit(solution)/shard_map/pallas_call | solution.py:252
Async XLA Ops:
  0.6 9.6 %copy-start.3 = (bf16[512,512]{1,0:T(8,128)(2,1)S(1)}, bf16[512,512]{1,0:T(8,128)(2,1)}, u32[]{:S(2)}) copy-start(bf16[512,512]{1,0:T(8,128)(2,1)} %q_ref.5) | copy-start | bytes 1572868
  0.6 55.3 %collective-permute-start.4 = (bf16[512,2048]{1,0:T(8,128)(2,1)}, bf16[512,2048]{1,0:T(8,128)(2,1)S(1)}, u32[]{:S(2)}, u32[]{:S(2)}) collective-permute-start(bf16[512,2048]{1,0:T(8,128)(2,1)} %own_ref.3), channel_id=1, source_target_pairs={{0,16},{16,0},{1,17},{17,1},{2,18},{18,2},{3,19},{19,3},{4,20},{20... | collective-permute-start | bytes 6291464 | tf_op jit(solution)/shard_map/ppermute | solution.py:305
  1.2 1.0 %copy-start.4 = (bf16[512,512]{1,0:T(8,128)(2,1)S(1)}, bf16[512,512]{1,0:T(8,128)(2,1)}, u32[]{:S(2)}) copy-start(bf16[512,512]{1,0:T(8,128)(2,1)} %k_ref.5) | copy-start | bytes 1572868
  2.2 1.0 %copy-start.6 = (bf16[512,512]{1,0:T(8,128)(2,1)S(1)}, bf16[512,512]{1,0:T(8,128)(2,1)}, u32[]{:S(2)}) copy-start(bf16[512,512]{1,0:T(8,128)(2,1)} %v_ref.5) | copy-start | bytes 1572868
  3.2 7.0 %copy-start.5 = (bf16[512,512]{1,0:T(8,128)(2,1)S(1)}, bf16[512,512]{1,0:T(8,128)(2,1)}, u32[]{:S(2)}) copy-start(bf16[512,512]{1,0:T(8,128)(2,1)} %k_ref.5) | copy-start | bytes 1572868
  3.8 6.4 %collective-permute-start = (bf16[512,128]{1,0:T(8,128)(2,1)S(1)}, bf16[512,128]{1,0:T(8,128)(2,1)S(1)}, u32[]{:S(2)}, u32[]{:S(2)}) collective-permute-start(bf16[512,128]{1,0:T(8,128)(2,1)S(1)} %shard_map.92), channel_id=1, source_target_pairs={{0,16},{1,17},{2,18},{3,19},{4,20},{5,21},{6,22},{7,23},{8,24},{9,... | collective-permute-start | bytes 393224 | tf_op jit(solution)/shard_map/ppermute | solution.py:305
  5.8 4.4 %copy-start.7 = (bf16[512,512]{1,0:T(8,128)(2,1)S(1)}, bf16[512,512]{1,0:T(8,128)(2,1)}, u32[]{:S(2)}) copy-start(bf16[512,512]{1,0:T(8,128)(2,1)} %v_ref.5) | copy-start | bytes 1572868
  7.2 11.2 %collective-permute-start.5 = (bf16[256,1024]{1,0:T(8,128)(2,1)S(1)}, bf16[256,1024]{1,0:T(8,128)(2,1)S(1)}, u32[]{:S(2)}, u32[]{:S(2)}) collective-permute-start(bf16[256,1024]{1,0:T(8,128)(2,1)S(1)} %get-tuple-element.24), channel_id=1, source_target_pairs={{0,4},{4,0},{24,12},{28,8},{16,24},{20,28},{8,16},{12,20},{1,5},{5... | collective-permute-start | bytes 1572872 | tf_op jit(solution)/shard_map/ppermute | solution.py:332
  11.8 2.2 %copy-start = (bf16[512,4096]{1,0:T(8,128)(2,1)S(1)}, bf16[512,4096]{1,0:T(8,128)(2,1)}, u32[]{:S(2)}) copy-start(bf16[512,4096]{1,0:T(8,128)(2,1)} %grad_ref.5) | copy-start | bytes 12582916
  14.0 42.5 %copy-start.1 = (bf16[512,4096]{1,0:T(8,128)(2,1)S(1)}, bf16[512,4096]{1,0:T(8,128)(2,1)}, u32[]{:S(2)}) copy-start(bf16[512,4096]{1,0:T(8,128)(2,1)} %grad_ref.5) | copy-start | bytes 12582916
  14.0 42.5 %copy-start.2 = (bf16[512,2048]{1,0:T(8,128)(2,1)S(1)}, bf16[512,2048]{1,0:T(8,128)(2,1)}, u32[]{:S(2)}) copy-start(bf16[512,2048]{1,0:T(8,128)(2,1)} %own_ref.3) | copy-start | bytes 6291460
  16.4 52.1 %collective-permute-start.14 = (bf16[512,2048]{1,0:T(8,128)(2,1)S(1)}, bf16[512,2048]{1,0:T(8,128)(2,1)S(1)}, u32[]{:S(2)}, u32[]{:S(2)}) collective-permute-start(bf16[512,2048]{1,0:T(8,128)(2,1)S(1)} %shard_map.97), channel_id=1, source_target_pairs={{0,16},{16,0},{1,17},{17,1},{2,18},{18,2},{3,19},{19,3},{4,20},{20... | collective-permute-start | bytes 6291464 | tf_op jit(solution)/shard_map/ppermute | solution.py:305
  16.4 16.5 %collective-permute-start.9 = (bf16[256,1024]{1,0:T(8,128)(2,1)S(1)}, bf16[256,1024]{1,0:T(8,128)(2,1)S(1)}, u32[]{:S(2)}, u32[]{:S(2)}) collective-permute-start(bf16[256,1024]{1,0:T(8,128)(2,1)S(1)} %get-tuple-element.23), channel_id=1, source_target_pairs={{16,12},{20,8},{8,4},{12,0},{17,13},{21,9},{9,5},{13,1},{18,14},{2... | collective-permute-start | bytes 1572872 | tf_op jit(solution)/shard_map/ppermute | solution.py:333
  17.7 16.8 %collective-permute-start.1 = (bf16[512,512]{1,0:T(8,128)(2,1)S(1)}, bf16[512,512]{1,0:T(8,128)(2,1)S(1)}, u32[]{:S(2)}, u32[]{:S(2)}) collective-permute-start(bf16[512,512]{1,0:T(8,128)(2,1)S(1)} %get-tuple-element.14.a_ref.attn_ref), channel_id=1, source_target_pairs={{0,4},{4,0},{8,12},{12,8},{16,24},{20,28},{24,16},{28,20},{1,5},{5... | collective-permute-start | bytes 1572872 | tf_op jit(solution)/shard_map/ppermute | solution.py:347
  18.4 21.2 %collective-permute-start.2 = (bf16[512,512]{1,0:T(8,128)(2,1)S(1)}, bf16[512,512]{1,0:T(8,128)(2,1)S(1)}, u32[]{:S(2)}, u32[]{:S(2)}) collective-permute-start(bf16[512,512]{1,0:T(8,128)(2,1)S(1)} %get-tuple-element.14.a_ref.attn_ref), channel_id=1, source_target_pairs={{0,8},{4,12},{8,0},{12,4},{16,20},{20,16},{24,28},{28,24},{1,9},{5... | collective-permute-start | bytes 1572872 | tf_op jit(solution)/shard_map/ppermute | solution.py:348
  33.0 14.2 %collective-permute-start.6 = (bf16[256,1024]{1,0:T(8,128)(2,1)S(1)}, bf16[256,1024]{1,0:T(8,128)(2,1)S(1)}, u32[]{:S(2)}, u32[]{:S(2)}) collective-permute-start(bf16[256,1024]{1,0:T(8,128)(2,1)S(1)} %collective-permute-done.5.m1_ref), channel_id=1, source_target_pairs={{0,1},{1,0},{2,3},{3,2},{4,5},{5,4},{6,7},{7,6},{8,9},{9,8},{10,11... | collective-permute-start | bytes 1572872 | tf_op jit(solution)/shard_map/ppermute | solution.py:349
  34.6 12.6 %collective-permute-start.7 = (bf16[256,1024]{1,0:T(8,128)(2,1)S(1)}, bf16[256,1024]{1,0:T(8,128)(2,1)S(1)}, u32[]{:S(2)}, u32[]{:S(2)}) collective-permute-start(bf16[256,1024]{1,0:T(8,128)(2,1)S(1)} %collective-permute-done.5.m1_ref), channel_id=1, source_target_pairs={{0,16},{16,0},{1,17},{17,1},{2,18},{18,2},{3,19},{19,3},{4,20},{20... | collective-permute-start | bytes 1572872 | tf_op jit(solution)/shard_map/ppermute | solution.py:352
  39.6 16.3 %collective-permute-start.10 = (bf16[256,1024]{1,0:T(8,128)(2,1)S(1)}, bf16[256,1024]{1,0:T(8,128)(2,1)S(1)}, u32[]{:S(2)}, u32[]{:S(2)}) collective-permute-start(bf16[256,1024]{1,0:T(8,128)(2,1)S(1)} %collective-permute-done.9.d_ref), channel_id=1, source_target_pairs={{0,1},{1,0},{2,3},{3,2},{4,5},{5,4},{6,7},{7,6},{8,9},{9,8},{10,11... | collective-permute-start | bytes 1572872 | tf_op jit(solution)/shard_map/ppermute | solution.py:350
  47.1 15.0 %collective-permute-start.11 = (bf16[256,1024]{1,0:T(8,128)(2,1)S(1)}, bf16[256,1024]{1,0:T(8,128)(2,1)S(1)}, u32[]{:S(2)}, u32[]{:S(2)}) collective-permute-start(bf16[256,1024]{1,0:T(8,128)(2,1)S(1)} %collective-permute-done.9.d_ref), channel_id=1, source_target_pairs={{0,16},{16,0},{1,17},{17,1},{2,18},{18,2},{3,19},{19,3},{4,20},{20... | collective-permute-start | bytes 1572872 | tf_op jit(solution)/shard_map/ppermute | solution.py:354
  47.1 16.5 %collective-permute-start.3 = (bf16[512,512]{1,0:T(8,128)(2,1)S(1)}, bf16[512,512]{1,0:T(8,128)(2,1)S(1)}, u32[]{:S(2)}, u32[]{:S(2)}) collective-permute-start(bf16[512,512]{1,0:T(8,128)(2,1)S(1)} %collective-permute-done.1.a1_ref), channel_id=1, source_target_pairs={{0,8},{4,12},{8,0},{12,4},{16,20},{20,16},{24,28},{28,24},{1,9},{5... | collective-permute-start | bytes 1572872 | tf_op jit(solution)/shard_map/ppermute | solution.py:351
  55.9 7.7 %collective-permute-start.8 = (bf16[256,1024]{1,0:T(8,128)(2,1)S(1)}, bf16[256,1024]{1,0:T(8,128)(2,1)S(1)}, u32[]{:S(2)}, u32[]{:S(2)}) collective-permute-start(bf16[256,1024]{1,0:T(8,128)(2,1)S(1)} %collective-permute-done.6.z1_ref), channel_id=1, source_target_pairs={{0,16},{16,0},{1,17},{17,1},{2,18},{18,2},{3,19},{19,3},{4,20},{20... | collective-permute-start | bytes 1572872 | tf_op jit(solution)/shard_map/ppermute | solution.py:353
  55.9 7.7 %collective-permute-start.12 = (bf16[256,1024]{1,0:T(8,128)(2,1)S(1)}, bf16[256,1024]{1,0:T(8,128)(2,1)S(1)}, u32[]{:S(2)}, u32[]{:S(2)}) collective-permute-start(bf16[256,1024]{1,0:T(8,128)(2,1)S(1)} %collective-permute-done.10.dz_ref), channel_id=1, source_target_pairs={{0,16},{16,0},{1,17},{17,1},{2,18},{18,2},{3,19},{19,3},{4,20},{20... | collective-permute-start | bytes 1572872 | tf_op jit(solution)/shard_map/ppermute | solution.py:355
  62.1 10.0 %collective-permute-start.13 = (bf16[512,128]{1,0:T(8,128)(2,1)S(1)}, bf16[512,128]{1,0:T(8,128)(2,1)S(1)}, u32[]{:S(2)}, u32[]{:S(2)}) collective-permute-start(bf16[512,128]{1,0:T(8,128)(2,1)S(1)} %get-tuple-element.18), channel_id=1, source_target_pairs={{16,0},{17,1},{18,2},{19,3},{20,4},{21,5},{22,6},{23,7},{24,8},{25... | collective-permute-start | bytes 393224 | tf_op jit(solution)/shard_map/ppermute | solution.py:305
